TPU v7x, 512 devices: a whole 4x4x16 slice. The times are simulated.
512 devices in a mesh: seq: 32 (over x, y, core), exp: 16 (over z).
Axes of the slice: x: 4, y: 4, z: 16, core: 2. Of those that a mesh axis runs over, the one named last changes fastest.
Arguments:
- hidden_in: bfloat16 [16, 4096, 2048], P('exp', 'seq'), may hold values from -6 to 6
- route_ids: int32 [16, 4096, 2], P('exp', 'seq'), may hold values from 0 to 15, all different within a row; in each aligned block of 128 rows (0 to 127, 128 to 255, ..., all dimensions but the last counted through in order) at most 32 rows name the same one
- route_gates: float32 [16, 4096, 2], P('exp', 'seq'), may hold values from 0.1 to 1
- language: int32 [16, 4096], P('exp', 'seq'), may hold values from 0 to 7
- allowed: int32 [8, 8], replicated, may hold values from 0 to 15, all different within a row
- w_gate: bfloat16 [16, 2048, 512], P('exp', 'seq'), may hold values from -0.125 to 0.125
- w_up: bfloat16 [16, 2048, 512], P('exp', 'seq'), may hold values from -0.125 to 0.125
- w_down: bfloat16 [16, 512, 2048], P('exp', 'seq'), may hold values from -0.25 to 0.25
- gate_proj: bfloat16 [2048, 64], replicated, may hold values from -0.125 to 0.125
- head_decay: float32 [32], replicated, may hold values from -13 to -2
- query_in: bfloat16 [16, 4096, 2048], P('exp', 'seq'), may hold values from -6 to 6
- key_in: bfloat16 [16, 4096, 2048], P('exp', 'seq'), may hold values from -6 to 6
- value_in: bfloat16 [16, 4096, 4096], P('exp', 'seq'), may hold values from -6 to 6
- block_inverse: bfloat16 [16, 4096, 2048], P('exp', 'seq'), may hold values from -0.29882812 to 0.29882812
Outputs:
- routed: bfloat16 [16, 4096, 2048], P('exp', 'seq')
- core_out: bfloat16 [16, 4096, 4096], P('exp', 'seq')
Inputs may be any that keep to these rules, and one draw needn't show every extreme that they name: `route_ids`: among the routes of the rows of one device, no expert is named more than 32 times, a bound that some block reaches. `allowed`: each of its rows names 8 different experts, and every expert is allowed for some language.
All inputs are finite; a program needn't handle non-finite values.
Results may differ from a plain program's by a relative error of at most 0.019.
Values may be sent and summed in bfloat16 or wider, within the bound.
A program may use at most 64 MiB of HBM per device.

v0:
```python
import jax
import jax.numpy as jnp
from jax import lax
from jax.sharding import PartitionSpec as P

highest = lax.Precision.HIGHEST


def normalized(values, head_count, factor_scale):
    flat_vals = values.astype(jnp.float32)
    shaped = flat_vals.reshape(flat_vals.shape[0], head_count, -1)
    factor = lax.rsqrt(jnp.sum(shaped * shaped, axis=-1, keepdims=True) + 1e-06) * factor_scale
    return (shaped * factor).astype(jnp.bfloat16)


def delta_blocks(queries, key_rows, values, inverse, beta_gate, decay_log):
    head_count, block_count, block_size, key_dim = queries.shape
    value_dim = values.shape[-1]
    cumulative = jnp.cumsum(decay_log, axis=-1)
    eye_mat = jnp.eye(block_size, dtype=jnp.float32)
    strict = jnp.tril(jnp.ones((block_size, block_size), jnp.float32), -1)
    causal = jnp.tril(jnp.ones((block_size, block_size), jnp.bool_))
    solver = (eye_mat + strict * inverse.astype(jnp.float32)).astype(jnp.bfloat16)
    beta_vals = (beta_gate[..., None] * values.astype(jnp.float32)).astype(jnp.bfloat16)
    beta_keys = (
        (beta_gate * jnp.exp(cumulative))[..., None] * key_rows.astype(jnp.float32)
    ).astype(jnp.bfloat16)
    new_base = jnp.einsum("hnij,hnjd->hnid", solver, beta_vals, preferred_element_type=jnp.float32)
    key_mix = jnp.einsum("hnij,hnjd->hnid", solver, beta_keys, preferred_element_type=jnp.float32)
    query_gate = queries.astype(jnp.float32) * jnp.exp(cumulative)[..., None]
    spread = jnp.where(causal, cumulative[..., :, None] - cumulative[..., None, :], 0.0)
    scores = jnp.einsum("hnid,hnjd->hnij", queries, key_rows, preferred_element_type=jnp.float32)
    weights = jnp.where(causal, scores * jnp.exp(spread), 0.0).astype(jnp.bfloat16)
    tail_decay = jnp.exp(cumulative[..., -1:] - cumulative)
    key_decay = (key_rows.astype(jnp.float32) * tail_decay[..., None]).astype(jnp.bfloat16)
    carry_decay = jnp.exp(cumulative[..., -1])

    def advance(carry_state, inputs):
        mix_now, base_now, gate_now, keyd_now, keep_now = inputs
        fresh_vals = (
            base_now - jnp.einsum("hid,hde->hie", mix_now, carry_state, precision=highest)
        ).astype(jnp.bfloat16)
        early_out = jnp.einsum("hid,hde->hie", gate_now, carry_state, precision=highest)
        carry_state = keep_now[:, None, None] * carry_state + jnp.einsum(
            "hid,hie->hde", keyd_now, fresh_vals, preferred_element_type=jnp.float32
        )
        return (carry_state, (fresh_vals, early_out))

    moved_seq = tuple(
        (
            jnp.moveaxis(element, 1, 0)
            for element in (key_mix, new_base, query_gate, key_decay, carry_decay)
        )
    )
    initial = jnp.zeros((head_count, key_dim, value_dim), jnp.float32)
    _, (fresh_vals, early_out) = lax.scan(advance, initial, moved_seq)
    fresh_vals = jnp.moveaxis(fresh_vals, 0, 1)
    early_out = jnp.moveaxis(early_out, 0, 1)
    local_out = jnp.einsum(
        "hnij,hnjd->hnid", weights, fresh_vals, preferred_element_type=jnp.float32
    )
    return (early_out + local_out).astype(jnp.bfloat16)


def per_device(
    hidden_in,
    route_ids,
    route_gates,
    language,
    allowed,
    w_gate,
    w_up,
    w_down,
    gate_proj,
    head_decay,
    query_in,
    key_in,
    value_in,
    block_inverse,
):
    exp_size = lax.axis_size("exp")
    seq_size = lax.axis_size("seq")
    tokens = hidden_in[0]
    tok_rows, model_width = tokens.shape
    routes_tok = route_ids.shape[2]
    experts = exp_size * w_gate.shape[0]
    capacity = 2 * tok_rows * routes_tok // experts
    flat_routes = route_ids[0].reshape(-1)
    expert_range = jnp.arange(experts, dtype=jnp.int32)
    onehot = (flat_routes[:, None] == expert_range[None, :]).astype(jnp.int32)
    earlier = jnp.cumsum(onehot, axis=0) - onehot
    slot_index = jnp.sum(earlier * onehot, axis=1)
    target = flat_routes * capacity + slot_index
    route_token = jnp.arange(tok_rows * routes_tok, dtype=jnp.int32) // routes_tok
    source_row = jnp.full((experts * capacity,), tok_rows, jnp.int32).at[target].set(route_token)
    padded = jnp.concatenate([tokens, jnp.zeros((1, model_width), tokens.dtype)], axis=0)
    outgoing = jnp.take(padded, source_row, axis=0).reshape(experts, capacity, model_width)
    incoming = lax.all_to_all(outgoing, "exp", split_axis=0, concat_axis=0, tiled=True)
    expert_rows = incoming.reshape(-1, model_width)

    def add_rows(portion):
        return jnp.dot(expert_rows, portion, preferred_element_type=jnp.float32)

    gate_proj_h = add_rows(lax.all_gather(w_gate[0], "seq", axis=0, tiled=True))
    up_proj_h = add_rows(lax.all_gather(w_up[0], "seq", axis=0, tiled=True))
    hidden = (jax.nn.silu(gate_proj_h) * up_proj_h).astype(jnp.bfloat16)
    produced = jnp.dot(
        hidden,
        lax.all_gather(w_down[0], "seq", axis=0, tiled=True),
        preferred_element_type=jnp.float32,
    )
    produced = produced.astype(jnp.bfloat16).reshape(exp_size, -1, model_width)
    returned = lax.all_to_all(produced, "exp", split_axis=0, concat_axis=0, tiled=True)
    back_rows = jnp.take(returned.reshape(-1, model_width), target, axis=0).reshape(
        tok_rows, routes_tok, model_width
    )
    lang_count = allowed.shape[0]
    lang_table = jnp.any(allowed[:, :, None] == expert_range[None, None, :], axis=1).astype(
        jnp.float32
    )
    lang_hot = (language[0][:, None] == jnp.arange(lang_count, dtype=jnp.int32)[None, :]).astype(
        jnp.float32
    )
    token_allow = jnp.dot(lang_hot, lang_table, precision=highest)
    route_allow = jnp.sum(
        token_allow[:, None, :] * onehot.reshape(tok_rows, routes_tok, experts).astype(jnp.float32),
        axis=2,
    )
    route_weight = route_gates[0] * route_allow
    mixed = jnp.sum(route_weight[..., None] * back_rows.astype(jnp.float32), axis=1)
    routed = mixed.astype(jnp.bfloat16)
    residual = (tokens.astype(jnp.float32) + routed.astype(jnp.float32)).astype(jnp.bfloat16)
    logits = jnp.dot(residual, gate_proj, preferred_element_type=jnp.float32).astype(jnp.bfloat16)
    heads_v = head_decay.shape[0]
    heads_k = heads_v // 2
    key_dim = query_in.shape[2] // heads_k
    heads_dev = heads_v // seq_size
    beta_logit = logits[:, :heads_v]
    decay_logit = logits[:, heads_v:]
    queries = query_in[0]
    key_rows = key_in[0]
    values_in = value_in[0]
    inverse_in = block_inverse[0]

    def repeated(values):
        return jnp.repeat(values.reshape(tok_rows, heads_k, key_dim), 2, axis=1).reshape(
            tok_rows, -1
        )

    full_q, full_k, got_v, got_inv, got_beta, got_decay = (
        lax.all_to_all(repeated(queries), "seq", split_axis=1, concat_axis=0, tiled=True),
        lax.all_to_all(repeated(key_rows), "seq", split_axis=1, concat_axis=0, tiled=True),
        lax.all_to_all(values_in, "seq", split_axis=1, concat_axis=0, tiled=True),
        lax.all_to_all(inverse_in, "seq", split_axis=1, concat_axis=0, tiled=True),
        lax.all_to_all(beta_logit, "seq", split_axis=1, concat_axis=0, tiled=True),
        lax.all_to_all(decay_logit, "seq", split_axis=1, concat_axis=0, tiled=True),
    )
    seq_len = full_q.shape[0]
    block_size = inverse_in.shape[1] // heads_v
    block_count = seq_len // block_size
    query_n = normalized(full_q, heads_dev, key_dim ** (-0.5))
    key_n = normalized(full_k, heads_dev, 0.5)

    def arrange(values):
        return values.reshape(block_count, block_size, heads_dev, -1).transpose(2, 0, 1, 3)

    head_start = lax.axis_index("seq") * heads_dev
    decay_rate = jnp.exp(lax.dynamic_slice_in_dim(head_decay, head_start, heads_dev))
    beta_gate = jax.nn.sigmoid(got_beta.astype(jnp.float32))
    decay_log = -decay_rate[None, :] * jax.nn.softplus(got_decay.astype(jnp.float32))
    result = delta_blocks(
        arrange(query_n),
        arrange(key_n),
        arrange(got_v.reshape(seq_len, heads_dev, -1)),
        arrange(got_inv.reshape(seq_len, heads_dev, block_size)),
        beta_gate.reshape(block_count, block_size, heads_dev).transpose(2, 0, 1),
        decay_log.reshape(block_count, block_size, heads_dev).transpose(2, 0, 1),
    )
    flat_out = result.transpose(1, 2, 0, 3).reshape(seq_len, -1)
    core_out = lax.all_to_all(flat_out, "seq", split_axis=0, concat_axis=1, tiled=True)
    return (routed[None], core_out[None])


def solution(mesh):
    in_specs = (
        P("exp", "seq", None),
        P("exp", "seq", None),
        P("exp", "seq", None),
        P("exp", "seq"),
        P(),
        P("exp", "seq", None),
        P("exp", "seq", None),
        P("exp", "seq", None),
        P(),
        P(),
        P("exp", "seq", None),
        P("exp", "seq", None),
        P("exp", "seq", None),
        P("exp", "seq", None),
    )
    out_specs = (P("exp", "seq", None), P("exp", "seq", None))
    return jax.shard_map(
        per_device, mesh=mesh, in_specs=in_specs, out_specs=out_specs, check_vma=False
    )
```

profile of v0, /device:TPU:33, one launch (start us, length us, event | category | flops | bytes accessed | tf_op | source)
XLA Modules:
  0.0 757.4 jit_solution(230179408285907515)
XLA Ops:
  7.9 2.0 copy.125
  10.0 7.8 %all-to-all-start.4 = ((bf16[128,32,64]{0,2,1:T(8,128)(2,1)}), bf16[128,32,64]{0,2,1:T(8,128)(2,1)S(1)}, u32[]{:S(2)}, u32[]{:S(2)}) async-start(bf16[128,32,64]{0,2,1:T(8,128)(2,1)} %bitcast.23), calls=%async_computation.4 | async-start | bytes 1048576 | tf_op jit(solution)/shard_map/all_to_all | solution.py:154
  21.0 8.3 %all-to-all-done.4 = bf16[128,32,64]{0,2,1:T(8,128)(2,1)S(1)} async-done(((bf16[128,32,64]{0,2,1:T(8,128)(2,1)}), bf16[128,32,64]{0,2,1:T(8,128)(2,1)S(1)}, u32[]{:S(2)}, u32[]{:S(2)}) %all-to-all-start.4) | async-done | bytes 524320 | tf_op jit(solution)/shard_map/all_to_all | solution.py:154
  30.6 3.7 all-to-all-start.3
  34.5 3.3 gather_fusion
  37.8 3.2 broadcast_select_fusion
  41.0 10.8 %all-to-all-done.3 = bf16[128,32,128]{2,0,1:T(8,128)(2,1)S(1)} async-done(((bf16[128,32,128]{2,0,1:T(8,128)(2,1)}), bf16[128,32,128]{2,0,1:T(8,128)(2,1)S(1)}, u32[]{:S(2)}, u32[]{:S(2)}) %all-to-all-start.3) | async-done | bytes 1048608 | tf_op jit(solution)/shard_map/all_to_all | solution.py:152
  51.8 14.3 %all-to-all-start = ((bf16[16,32,2048]{2,1,0:T(8,128)(2,1)}), bf16[16,32,2048]{2,1,0:T(8,128)(2,1)}, u32[]{:S(2)}, u32[]{:S(2)}) async-start(bf16[16,32,2048]{2,1,0:T(8,128)(2,1)} %broadcast_select_fusion), calls=%async_computation | async-start | bytes 4194304 | tf_op jit(solution)/shard_map/all_to_all | solution.py:98
  67.9 90.8 %all-to-all-done = bf16[16,32,2048]{2,1,0:T(8,128)(2,1)} async-done(((bf16[16,32,2048]{2,1,0:T(8,128)(2,1)}), bf16[16,32,2048]{2,1,0:T(8,128)(2,1)}, u32[]{:S(2)}, u32[]{:S(2)}) %all-to-all-start) | async-done | bytes 2097184 | tf_op jit(solution)/shard_map/all_to_all | solution.py:98
  159.9 6.3 all-to-all-start.7
  166.3 3.5 fusion.26
  169.8 40.0 %all-gather.9.cloned.1.call-done = bf16[1,2048,512]{2,1,0:T(8,128)(2,1)} async-done(((bf16[1,64,512]{2,1,0:T(8,128)(2,1)}), bf16[1,2048,512]{2,1,0:T(8,128)(2,1)}) %all-gather.9.cloned.1.call-update) | async-done | bytes 2097168 | tf_op jit(solution)/shard_map/all_gather | solution.py:105
  209.8 6.7 convolution_convert_fusion
  217.4 12.1 %all-to-all-start.1 = ((bf16[16,32,2048]{2,1,0:T(8,128)(2,1)}), bf16[16,32,2048]{2,1,0:T(8,128)(2,1)S(1)}, u32[]{:S(2)}, u32[]{:S(2)}) async-start(bf16[16,32,2048]{2,1,0:T(8,128)(2,1)} %bitcast.187), calls=%async_computation.1 | async-start | bytes 4194304 | tf_op jit(solution)/shard_map/all_to_all | solution.py:113
  236.3 2.3 copy.129
  238.5 2.3 copy.130
  245.1 1.6 copy.126
  246.7 2.7 reshape.556
  249.3 3.0 add_convert_fusion
  252.3 2.9 copy.131
  256.5 65.6 %all-to-all-done.1 = bf16[16,32,2048]{2,1,0:T(8,128)(2,1)S(1)} async-done(((bf16[16,32,2048]{2,1,0:T(8,128)(2,1)}), bf16[16,32,2048]{2,1,0:T(8,128)(2,1)S(1)}, u32[]{:S(2)}, u32[]{:S(2)}) %all-to-all-start.1) | async-done | bytes 2097184 | tf_op jit(solution)/shard_map/all_to_all | solution.py:113
  322.1 7.7 %all-to-all-start.6 = ((bf16[128,32,128]{2,0,1:T(8,128)(2,1)}), bf16[128,32,128]{2,0,1:T(8,128)(2,1)}, u32[]{:S(2)}, u32[]{:S(2)}) async-start(bf16[128,32,128]{2,0,1:T(8,128)(2,1)} %copy.130), calls=%async_computation.6 | async-start | bytes 2097152 | tf_op jit(solution)/shard_map/all_to_all | solution.py:153
  329.8 2.4 multiply_reduce_fusion
  332.2 2.5 gather_fusion.1
  334.7 1.8 gather.15
  336.5 4.1 multiply_reduce_fusion.2
  342.4 4.4 all-to-all-done.6
  346.8 4.0 all-to-all-start.2
  351.7 2.8 convert_element_type.352
  354.6 2.9 convert_element_type.350
  358.1 7.4 all-to-all-start.5
  368.1 4.5 all-to-all-done.5
  374.8 3.7 convolution_bitcast_fusion.3
  378.5 2.5 convolution_bitcast_fusion.2
  381.0 3.7 convert_multiply_fusion
  384.7 339.8 %while.15 = (s32[]{:T(128)}, f32[1,128,128]{2,1,0:T(8,128)S(1)}, bf16[64,1,64,128]{3,2,1,0:T(8,128)(2,1)}, f32[64,1,64,128]{3,2,1,0:T(8,128)}, f32[64,1]{0,1:T(1...) while((s32[]{:T(128)}, f32[1,128,128]{2,1,0:T(8,128)S(1)}, ...), condition=%wide.region_11.12_spmd.clone, body=%wide.region_10.11_spmd.clone.sunk | while | flops 27361284 | bytes 461957 | solution.py:56
  384.7 1.6 bitcast_dynamic-update-slice_fusion.2
  432.5 1.6 bitcast_dynamic-update-slice_fusion.2
  453.7 1.6 bitcast_dynamic-update-slice_fusion.2
  459.0 1.6 bitcast_dynamic-update-slice_fusion.2
  480.3 1.6 bitcast_dynamic-update-slice_fusion.2
  517.4 1.6 bitcast_dynamic-update-slice_fusion.2
  544.0 1.6 bitcast_dynamic-update-slice_fusion.2
  623.6 1.6 bitcast_dynamic-update-slice_fusion.2
  704.8 1.6 fusion.81
  713.8 1.6 bitcast_dynamic-update-slice_fusion.2
  724.5 3.9 fusion.22
  728.3 20.6 %all_to_all.104 = bf16[32,128,128]{2,1,0:T(8,128)(2,1)S(1)} all-to-all(bf16[32,128,128]{2,1,0:T(8,128)(2,1)S(1)} %bitcast.184), channel_id=1, replica_groups=mesh['seq'=32,'exp'=16] {'seq'}, dimensions={0} | all-to-all | bytes 2097152 | tf_op jit(solution)/shard_map/all_to_all | solution.py:180
  (357 shorter events, 353.4 us)
Async XLA Ops:
  7.2 334.3 %copy-start = (bf16[2048,64]{0,1:T(8,128)(2,1)S(1)}, bf16[2048,64]{0,1:T(8,128)(2,1)}, u32[]{:S(2)}) copy-start(bf16[2048,64]{0,1:T(8,128)(2,1)} %param.24) | copy-start | bytes 786436
  7.2 10.6 %copy-start.15 = (s32[1,128,2]{1,2,0:T(2,128)S(1)}, s32[1,128,2]{1,2,0:T(2,128)}, u32[]{:S(2)}) copy-start(s32[1,128,2]{1,2,0:T(2,128)} %param.17) | copy-start | bytes 3076
  7.2 12.1 %copy-start.8 = (bf16[1,128,2048]{2,1,0:T(8,128)(2,1)S(1)}, bf16[1,128,2048]{2,1,0:T(8,128)(2,1)}, u32[]{:S(2)}) copy-start(bf16[1,128,2048]{2,1,0:T(8,128)(2,1)} %param.27) | copy-start | bytes 1572868
  7.2 159.1 %all-gather.7.cloned.1.call-start = ((), (), s32[]{:S(2)}) async-start(), calls=%async_computation.9 | async-start | bytes 2162688 | tf_op jit(solution)/shard_map/all_gather | solution.py:104
  10.0 19.4 %all-to-all-start.4 = ((bf16[128,32,64]{0,2,1:T(8,128)(2,1)}), bf16[128,32,64]{0,2,1:T(8,128)(2,1)S(1)}, u32[]{:S(2)}, u32[]{:S(2)}) async-start(bf16[128,32,64]{0,2,1:T(8,128)(2,1)} %bitcast.23), calls=%async_computation.4 | async-start | bytes 1048576 | tf_op jit(solution)/shard_map/all_to_all | solution.py:154
  19.5 14.9 %copy-start.6 = (bf16[1,128,2048]{2,1,0:T(8,128)(2,1)S(1)}, bf16[1,128,2048]{2,1,0:T(8,128)(2,1)}, u32[]{:S(2)}) copy-start(bf16[1,128,2048]{2,1,0:T(8,128)(2,1)} %param.16) | copy-start | bytes 1572868
  19.6 10.9 %copy-start.16 = (s32[256,1]{0,1:T(1,128)}, s32[256,1]{0,1:T(1,128)S(1)}, u32[]{:S(2)}) copy-start(s32[256,1]{0,1:T(1,128)S(1)} %compare_select_fusion.1) | copy-start | bytes 3076
  29.4 1.2 copy-start.4
  30.6 21.3 %all-to-all-start.3 = ((bf16[128,32,128]{2,0,1:T(8,128)(2,1)}), bf16[128,32,128]{2,0,1:T(8,128)(2,1)S(1)}, u32[]{:S(2)}, u32[]{:S(2)}) async-start(bf16[128,32,128]{2,0,1:T(8,128)(2,1)} %bitcast.18), calls=%async_computation.3 | async-start | bytes 2097152 | tf_op jit(solution)/shard_map/all_to_all | solution.py:152
  41.0 26.7 %copy-start.9 = (bf16[1,128,2048]{2,1,0:T(8,128)(2,1)S(1)}, bf16[1,128,2048]{2,1,0:T(8,128)(2,1)}, u32[]{:S(2)}) copy-start(bf16[1,128,2048]{2,1,0:T(8,128)(2,1)} %param.26) | copy-start | bytes 1572868
  51.8 106.9 %all-to-all-start = ((bf16[16,32,2048]{2,1,0:T(8,128)(2,1)}), bf16[16,32,2048]{2,1,0:T(8,128)(2,1)}, u32[]{:S(2)}, u32[]{:S(2)}) async-start(bf16[16,32,2048]{2,1,0:T(8,128)(2,1)} %broadcast_select_fusion), calls=%async_computation | async-start | bytes 4194304 | tf_op jit(solution)/shard_map/all_to_all | solution.py:98
  66.2 103.6 %all-gather.11.cloned.1.call-start = ((), (), s32[]{:S(2)}) async-start(), calls=%async_computation.11 | async-start | bytes 2162688 | tf_op jit(solution)/shard_map/all_gather | solution.py:109
  66.9 142.9 %all-gather.9.cloned.1.call-start = ((), (), s32[]{:S(2)}) async-start(), calls=%async_computation.10 | async-start | bytes 2162688 | tf_op jit(solution)/shard_map/all_gather | solution.py:105
  159.9 56.5 %all-to-all-start.7 = ((bf16[128,32,128]{2,0,1:T(8,128)(2,1)}), bf16[128,32,128]{2,0,1:T(8,128)(2,1)S(1)}, u32[]{:S(2)}, u32[]{:S(2)}) async-start(bf16[128,32,128]{2,0,1:T(8,128)(2,1)} %bitcast.35), calls=%async_computation.7 | async-start | bytes 2097152 | tf_op jit(solution)/shard_map/all_to_all | solution.py:151
  216.4 1.0 copy-start.2
  217.4 104.7 %all-to-all-start.1 = ((bf16[16,32,2048]{2,1,0:T(8,128)(2,1)}), bf16[16,32,2048]{2,1,0:T(8,128)(2,1)S(1)}, u32[]{:S(2)}, u32[]{:S(2)}) async-start(bf16[16,32,2048]{2,1,0:T(8,128)(2,1)} %bitcast.187), calls=%async_computation.1 | async-start | bytes 4194304 | tf_op jit(solution)/shard_map/all_to_all | solution.py:113
  322.1 24.6 %all-to-all-start.6 = ((bf16[128,32,128]{2,0,1:T(8,128)(2,1)}), bf16[128,32,128]{2,0,1:T(8,128)(2,1)}, u32[]{:S(2)}, u32[]{:S(2)}) async-start(bf16[128,32,128]{2,0,1:T(8,128)(2,1)} %copy.130), calls=%async_computation.6 | async-start | bytes 2097152 | tf_op jit(solution)/shard_map/all_to_all | solution.py:153
  334.7 6.7 copy-start.7
  334.7 16.0 %copy-start.12 = (f32[128,32]{0,1:T(8,128)S(1)}, f32[128,32]{0,1:T(8,128)}, u32[]{:S(2)}) copy-start(f32[128,32]{0,1:T(8,128)} %multiply_reduce_fusion) | copy-start | bytes 49156
  334.7 16.0 %copy-start.13 = (f32[32,128]{1,0:T(8,128)S(1)}, f32[32,128]{1,0:T(8,128)}, u32[]{:S(2)}) copy-start(f32[32,128]{1,0:T(8,128)} %multiply_bitcast_fusion.1) | copy-start | bytes 49156
  340.6 0.8 copy-start.5
  346.8 11.3 %all-to-all-start.2 = ((bf16[128,32,1]{0,2,1:T(2,128)(2,1)}), bf16[128,32,1]{0,2,1:T(2,128)(2,1)S(1)}, u32[]{:S(2)}, u32[]{:S(2)}) async-start(bf16[128,32,1]{0,2,1:T(2,128)(2,1)} %copy.123), calls=%async_computation.2 | async-start | bytes 32768 | tf_op jit(solution)/shard_map/all_to_all | solution.py:156
  354.6 20.2 %copy-start.3 = (bf16[64,64,64]{2,1,0:T(8,128)(2,1)S(1)}, bf16[64,64,64]{2,1,0:T(8,128)(2,1)}, u32[]{:S(2)}) copy-start(bf16[64,64,64]{2,1,0:T(8,128)(2,1)} %copy.131) | copy-start | bytes 1572868
  358.1 14.4 %all-to-all-start.5 = ((bf16[128,32,1]{0,2,1:T(2,128)(2,1)}), bf16[128,32,1]{0,2,1:T(2,128)(2,1)}, u32[]{:S(2)}, u32[]{:S(2)}) async-start(bf16[128,32,1]{0,2,1:T(2,128)(2,1)} %copy.127), calls=%async_computation.5 | async-start | bytes 32768 | tf_op jit(solution)/shard_map/all_to_all | solution.py:155
  378.5 2.5 copy-start.1
  378.5 2.5 copy-start.10
  381.0 3.7 copy-start.17
  384.7 339.8 %copy-start.11 = (f32[64,64]{1,0:T(8,128)S(1)}, f32[64,64]{1,0:T(8,128)}, u32[]{:S(2)}) copy-start(f32[64,64]{1,0:T(8,128)} %mul.296) | copy-start | bytes 49156
  384.7 339.8 %copy-start.14 = (pred[64,64]{1,0:T(8,128)(4,1)S(1)}, pred[64,64]{1,0:T(8,128)(4,1)}, u32[]{:S(2)}) copy-start(pred[64,64]{1,0:T(8,128)(4,1)} %iota_compare_fusion.2) | copy-start | bytes 12292
Sparse Core Ops, SparseCore 0:
  11.2 70.7 all-gather.6
  85.1 58.4 all-gather.10
  146.7 63.0 all-gather.8
where the time goes:
time: 772 us; the launch traced here: 757 us
  matrix products  319 us (41%)
  waiting for transfers between devices  227 us (29%)
  local copies, waits for them, and re-layouts  77.4 us (10%)
  starting transfers between devices  63.4 us (8%)
  other arithmetic  34.6 us (4%)
  blocking collectives  20.6 us (3%)
  between operations  14.9 us (2%)
    dot_general x64, matrix products, advance(): jnp.einsum('hid,hde->hie', mix_now, carry_state, precision=highest)  100 us
    dot_general x64, matrix products, advance(): jnp.einsum('hid,hde->hie', gate_now, carry_state, precision=highest)  99.6 us
    dot_general x64, matrix products, advance(): jnp.einsum('hid,hie->hde', keyd_now, fresh_vals, preferred_element_type=j...  97.4 us
    all_to_all x1, waiting for transfers between devices, per_device(): lax.all_to_all(outgoing, 'exp', split_axis=0, concat_axis=0, tiled=True)  90.8 us
    all_to_all x1, waiting for transfers between devices, per_device(): lax.all_to_all(produced, 'exp', split_axis=0, concat_axis=0, tiled=True)  65.6 us
    dynamic_slice x64, local copies, waits for them, and re-layouts, delta_blocks(): _, (fresh_vals, early_out) = lax.scan(advance, initial, moved_seq)  41.1 us
    all_gather x1, waiting for transfers between devices, per_device(): up_proj_h = add_rows(lax.all_gather(w_up[0], 'seq', axis=0, tiled=True))  40 us
    all_to_all x1, blocking collectives, per_device(): lax.all_to_all(flat_out, 'seq', split_axis=0, concat_axis=1, tiled=True)  20.6 us
  transfers between devices with their start and end apart: 11, of which 7 were waited for; matrix products, arithmetic and copies ran while one was open for 10% of the time, Pallas kernels for 0%

commit v1 on v0

--- a/solution.py
+++ b/solution.py
@@ -151,7 +151,12 @@
         lax.all_to_all(repeated(queries), "seq", split_axis=1, concat_axis=0, tiled=True),
         lax.all_to_all(repeated(key_rows), "seq", split_axis=1, concat_axis=0, tiled=True),
         lax.all_to_all(values_in, "seq", split_axis=1, concat_axis=0, tiled=True),
-        lax.all_to_all(inverse_in, "seq", split_axis=1, concat_axis=0, tiled=True),
+        jnp.concatenate(
+            lax.all_to_all(
+                jnp.stack(jnp.split(inverse_in, lax.axis_size("seq"), axis=1)), "seq", 0, 0
+            ),
+            axis=0,
+        ),
         lax.all_to_all(beta_logit, "seq", split_axis=1, concat_axis=0, tiled=True),
         lax.all_to_all(decay_logit, "seq", split_axis=1, concat_axis=0, tiled=True),
     )

time: 772 us -> 772 us (level)
  local copies, waits for them, and re-layouts: 77.4 us -> 96.8 us
  waiting for transfers between devices: 227 us -> 212 us
    unnamed x41 -> x72, local copies, waits for them, and re-layouts: 6.49 us -> 24.6 us
    all_gather x1, waiting for transfers between devices: 40 us -> 22.5 us  [per_device(): up_proj_h = add_rows(lax.all_gather(w_up[0], 'seq', axis=0, tiled=True))]
  transfers between devices with their start and end apart: 11 -> 11, of which waited for: 7 -> 7; matrix products, arithmetic and copies ran while one was open for 10% -> 12% of each run, Pallas kernels for 0% -> 0%
where the time goes in v1:
time: 772 us; the launch traced here: 758 us
  matrix products  319 us (41%)
  waiting for transfers between devices  212 us (27%)
  local copies, waits for them, and re-layouts  96.8 us (13%)
  starting transfers between devices  60.5 us (8%)
  other arithmetic  33.5 us (4%)
  blocking collectives  20.6 us (3%)
  between operations  14.9 us (2%)
    dot_general x64, matrix products, advance(): jnp.einsum('hid,hde->hie', mix_now, carry_state, precision=highest)  100 us
    dot_general x64, matrix products, advance(): jnp.einsum('hid,hde->hie', gate_now, carry_state, precision=highest)  99.6 us
    dot_general x64, matrix products, advance(): jnp.einsum('hid,hie->hde', keyd_now, fresh_vals, preferred_element_type=j...  97.4 us
    all_to_all x1, waiting for transfers between devices, per_device(): lax.all_to_all(outgoing, 'exp', split_axis=0, concat_axis=0, tiled=True)  91.9 us
    all_to_all x1, waiting for transfers between devices, per_device(): lax.all_to_all(produced, 'exp', split_axis=0, concat_axis=0, tiled=True)  66.1 us
    dynamic_slice x64, local copies, waits for them, and re-layouts, delta_blocks(): _, (fresh_vals, early_out) = lax.scan(advance, initial, moved_seq)  41.1 us
    unnamed x72, local copies, waits for them, and re-layouts  24.6 us
    all_gather x1, waiting for transfers between devices, per_device(): up_proj_h = add_rows(lax.all_gather(w_up[0], 'seq', axis=0, tiled=True))  22.5 us
  transfers between devices with their start and end apart: 11, of which 7 were waited for; matrix products, arithmetic and copies ran while one was open for 12% of the time, Pallas kernels for 0%

profile of v1, /device:TPU:33, one launch (start us, length us, event | category | flops | bytes accessed | tf_op | source)
XLA Modules:
  0.0 757.8 jit_solution(14139185713661344212)
XLA Ops:
  28.7 7.8 %all-to-all-start.4 = ((bf16[32,128,64]{1,2,0:T(8,128)(2,1)}), bf16[32,128,64]{1,2,0:T(8,128)(2,1)S(1)}, u32[]{:S(2)}, u32[]{:S(2)}) async-start(bf16[32,128,64]{1,2,0:T(8,128)(2,1)} %constant_dynamic-update-slice_fusion), calls=%async_computation.4 | async-start | bytes 1048576 | tf_op jit(solution)/shard_map/all_to_all | solution.py:155
  39.7 8.8 %all-to-all-done.4 = bf16[32,128,64]{1,2,0:T(8,128)(2,1)S(1)} async-done(((bf16[32,128,64]{1,2,0:T(8,128)(2,1)}), bf16[32,128,64]{1,2,0:T(8,128)(2,1)S(1)}, u32[]{:S(2)}, u32[]{:S(2)}) %all-to-all-start.4) | async-done | bytes 524320 | tf_op jit(solution)/shard_map/all_to_all | solution.py:155
  49.7 3.7 all-to-all-start.3
  53.6 3.3 gather_fusion
  56.9 3.2 broadcast_select_fusion
  60.1 11.4 %all-to-all-done.3 = bf16[128,32,128]{2,0,1:T(8,128)(2,1)S(1)} async-done(((bf16[128,32,128]{2,0,1:T(8,128)(2,1)}), bf16[128,32,128]{2,0,1:T(8,128)(2,1)S(1)}, u32[]{:S(2)}, u32[]{:S(2)}) %all-to-all-start.3) | async-done | bytes 1048608 | tf_op jit(solution)/shard_map/all_to_all | solution.py:152
  71.5 15.4 %all-to-all-start = ((bf16[16,32,2048]{2,1,0:T(8,128)(2,1)}), bf16[16,32,2048]{2,1,0:T(8,128)(2,1)}, u32[]{:S(2)}, u32[]{:S(2)}) async-start(bf16[16,32,2048]{2,1,0:T(8,128)(2,1)} %broadcast_select_fusion), calls=%async_computation | async-start | bytes 4194304 | tf_op jit(solution)/shard_map/all_to_all | solution.py:98
  88.7 91.9 %all-to-all-done = bf16[16,32,2048]{2,1,0:T(8,128)(2,1)} async-done(((bf16[16,32,2048]{2,1,0:T(8,128)(2,1)}), bf16[16,32,2048]{2,1,0:T(8,128)(2,1)}, u32[]{:S(2)}, u32[]{:S(2)}) %all-to-all-start) | async-done | bytes 2097184 | tf_op jit(solution)/shard_map/all_to_all | solution.py:98
  181.8 5.0 all-to-all-start.7
  186.8 3.5 fusion.26
  190.3 22.5 %all-gather.9.cloned.1.call-done = bf16[1,2048,512]{2,1,0:T(8,128)(2,1)} async-done(((bf16[1,64,512]{2,1,0:T(8,128)(2,1)}), bf16[1,2048,512]{2,1,0:T(8,128)(2,1)}) %all-gather.9.cloned.1.call-update) | async-done | bytes 2097168 | tf_op jit(solution)/shard_map/all_gather | solution.py:105
  212.8 6.6 convolution_convert_fusion
  220.5 9.9 %all-to-all-start.1 = ((bf16[16,32,2048]{2,1,0:T(8,128)(2,1)}), bf16[16,32,2048]{2,1,0:T(8,128)(2,1)S(1)}, u32[]{:S(2)}, u32[]{:S(2)}) async-start(bf16[16,32,2048]{2,1,0:T(8,128)(2,1)} %bitcast.345), calls=%async_computation.1 | async-start | bytes 4194304 | tf_op jit(solution)/shard_map/all_to_all | solution.py:113
  237.1 2.3 copy.107
  239.3 2.3 copy.108
  244.7 2.3 copy.104
  247.0 2.7 reshape.551
  249.7 3.0 add_convert_fusion
  252.7 2.9 copy.109
  256.9 66.1 %all-to-all-done.1 = bf16[16,32,2048]{2,1,0:T(8,128)(2,1)S(1)} async-done(((bf16[16,32,2048]{2,1,0:T(8,128)(2,1)}), bf16[16,32,2048]{2,1,0:T(8,128)(2,1)S(1)}, u32[]{:S(2)}, u32[]{:S(2)}) %all-to-all-start.1) | async-done | bytes 2097184 | tf_op jit(solution)/shard_map/all_to_all | solution.py:113
  322.9 7.2 all-to-all-start.6
  330.2 2.4 multiply_reduce_fusion
  332.6 2.5 gather_fusion.1
  335.1 1.8 gather.15
  336.9 4.1 multiply_reduce_fusion.2
  342.8 4.4 all-to-all-done.6
  347.1 4.0 all-to-all-start.2
  352.1 2.8 convert_element_type.347
  355.0 2.9 convert_element_type.345
  358.5 7.4 all-to-all-start.5
  368.5 4.5 all-to-all-done.5
  375.2 3.7 convolution_bitcast_fusion.3
  378.9 2.5 convolution_bitcast_fusion.2
  381.4 3.7 convert_multiply_fusion
  385.1 339.7 %while.15 = (s32[]{:T(128)}, f32[1,128,128]{2,1,0:T(8,128)S(1)}, bf16[64,1,64,128]{3,2,1,0:T(8,128)(2,1)}, f32[64,1,64,128]{3,2,1,0:T(8,128)}, f32[64,1]{0,1:T(1...) while((s32[]{:T(128)}, f32[1,128,128]{2,1,0:T(8,128)S(1)}, ...), condition=%wide.region_11.12_spmd.clone, body=%wide.region_10.11_spmd.clone.sunk | while | flops 27361284 | bytes 461957 | solution.py:56
  385.1 1.6 bitcast_dynamic-update-slice_fusion.2
  390.4 1.6 bitcast_dynamic-update-slice_fusion.2
  432.9 1.6 bitcast_dynamic-update-slice_fusion.2
  459.4 1.6 bitcast_dynamic-update-slice_fusion.2
  480.7 1.6 bitcast_dynamic-update-slice_fusion.2
  517.8 1.6 bitcast_dynamic-update-slice_fusion.2
  544.4 1.6 bitcast_dynamic-update-slice_fusion.2
  624.0 1.6 bitcast_dynamic-update-slice_fusion.2
  655.8 1.6 bitcast_dynamic-update-slice_fusion.2
  705.2 1.6 fusion.81
  714.2 1.6 bitcast_dynamic-update-slice_fusion.2
  724.9 3.9 fusion.22
  728.7 20.6 %all_to_all.96 = bf16[32,128,128]{2,1,0:T(8,128)(2,1)S(1)} all-to-all(bf16[32,128,128]{2,1,0:T(8,128)(2,1)S(1)} %bitcast.310), channel_id=1, replica_groups=mesh['seq'=32,'exp'=16] {'seq'}, dimensions={0} | all-to-all | bytes 2097152 | tf_op jit(solution)/shard_map/all_to_all | solution.py:185
  (388 shorter events, 371.4 us)
Async XLA Ops:
  7.2 334.7 %copy-start = (bf16[2048,64]{0,1:T(8,128)(2,1)S(1)}, bf16[2048,64]{0,1:T(8,128)(2,1)}, u32[]{:S(2)}) copy-start(bf16[2048,64]{0,1:T(8,128)(2,1)} %param.24) | copy-start | bytes 786436
  7.2 29.3 %copy-start.15 = (s32[1,128,2]{1,2,0:T(2,128)S(1)}, s32[1,128,2]{1,2,0:T(2,128)}, u32[]{:S(2)}) copy-start(s32[1,128,2]{1,2,0:T(2,128)} %param.17) | copy-start | bytes 3076
  7.2 30.8 %copy-start.8 = (bf16[1,128,2048]{2,1,0:T(8,128)(2,1)S(1)}, bf16[1,128,2048]{2,1,0:T(8,128)(2,1)}, u32[]{:S(2)}) copy-start(bf16[1,128,2048]{2,1,0:T(8,128)(2,1)} %param.27) | copy-start | bytes 1572868
  7.2 179.6 %all-gather.7.cloned.1.call-start = ((), (), s32[]{:S(2)}) async-start(), calls=%async_computation.9 | async-start | bytes 2162688 | tf_op jit(solution)/shard_map/all_gather | solution.py:104
  28.7 19.8 %all-to-all-start.4 = ((bf16[32,128,64]{1,2,0:T(8,128)(2,1)}), bf16[32,128,64]{1,2,0:T(8,128)(2,1)S(1)}, u32[]{:S(2)}, u32[]{:S(2)}) async-start(bf16[32,128,64]{1,2,0:T(8,128)(2,1)} %constant_dynamic-update-slice_fusion), calls=%async_computation.4 | async-start | bytes 1048576 | tf_op jit(solution)/shard_map/all_to_all | solution.py:155
  38.2 15.3 %copy-start.6 = (bf16[1,128,2048]{2,1,0:T(8,128)(2,1)S(1)}, bf16[1,128,2048]{2,1,0:T(8,128)(2,1)}, u32[]{:S(2)}) copy-start(bf16[1,128,2048]{2,1,0:T(8,128)(2,1)} %param.16) | copy-start | bytes 1572868
  38.3 11.4 %copy-start.16 = (s32[256,1]{0,1:T(1,128)}, s32[256,1]{0,1:T(1,128)S(1)}, u32[]{:S(2)}) copy-start(s32[256,1]{0,1:T(1,128)S(1)} %compare_select_fusion.1) | copy-start | bytes 3076
  48.5 1.2 copy-start.4
  49.7 21.8 %all-to-all-start.3 = ((bf16[128,32,128]{2,0,1:T(8,128)(2,1)}), bf16[128,32,128]{2,0,1:T(8,128)(2,1)S(1)}, u32[]{:S(2)}, u32[]{:S(2)}) async-start(bf16[128,32,128]{2,0,1:T(8,128)(2,1)} %bitcast.18), calls=%async_computation.3 | async-start | bytes 2097152 | tf_op jit(solution)/shard_map/all_to_all | solution.py:152
  60.1 28.3 %copy-start.9 = (bf16[1,128,2048]{2,1,0:T(8,128)(2,1)S(1)}, bf16[1,128,2048]{2,1,0:T(8,128)(2,1)}, u32[]{:S(2)}) copy-start(bf16[1,128,2048]{2,1,0:T(8,128)(2,1)} %param.26) | copy-start | bytes 1572868
  71.5 109.1 %all-to-all-start = ((bf16[16,32,2048]{2,1,0:T(8,128)(2,1)}), bf16[16,32,2048]{2,1,0:T(8,128)(2,1)}, u32[]{:S(2)}, u32[]{:S(2)}) async-start(bf16[16,32,2048]{2,1,0:T(8,128)(2,1)} %broadcast_select_fusion), calls=%async_computation | async-start | bytes 4194304 | tf_op jit(solution)/shard_map/all_to_all | solution.py:98
  86.9 103.4 %all-gather.11.cloned.1.call-start = ((), (), s32[]{:S(2)}) async-start(), calls=%async_computation.11 | async-start | bytes 2162688 | tf_op jit(solution)/shard_map/all_gather | solution.py:109
  87.7 125.2 %all-gather.9.cloned.1.call-start = ((), (), s32[]{:S(2)}) async-start(), calls=%async_computation.10 | async-start | bytes 2162688 | tf_op jit(solution)/shard_map/all_gather | solution.py:105
  181.8 37.7 %all-to-all-start.7 = ((bf16[128,32,128]{2,0,1:T(8,128)(2,1)}), bf16[128,32,128]{2,0,1:T(8,128)(2,1)S(1)}, u32[]{:S(2)}, u32[]{:S(2)}) async-start(bf16[128,32,128]{2,0,1:T(8,128)(2,1)} %bitcast.66), calls=%async_computation.7 | async-start | bytes 2097152 | tf_op jit(solution)/shard_map/all_to_all | solution.py:151
  219.5 1.0 copy-start.2
  220.5 102.4 %all-to-all-start.1 = ((bf16[16,32,2048]{2,1,0:T(8,128)(2,1)}), bf16[16,32,2048]{2,1,0:T(8,128)(2,1)S(1)}, u32[]{:S(2)}, u32[]{:S(2)}) async-start(bf16[16,32,2048]{2,1,0:T(8,128)(2,1)} %bitcast.345), calls=%async_computation.1 | async-start | bytes 4194304 | tf_op jit(solution)/shard_map/all_to_all | solution.py:113
  322.9 24.2 %all-to-all-start.6 = ((bf16[128,32,128]{2,0,1:T(8,128)(2,1)}), bf16[128,32,128]{2,0,1:T(8,128)(2,1)}, u32[]{:S(2)}, u32[]{:S(2)}) async-start(bf16[128,32,128]{2,0,1:T(8,128)(2,1)} %copy.108), calls=%async_computation.6 | async-start | bytes 2097152 | tf_op jit(solution)/shard_map/all_to_all | solution.py:153
  335.1 6.7 copy-start.7
  335.1 16.0 %copy-start.12 = (f32[128,32]{0,1:T(8,128)S(1)}, f32[128,32]{0,1:T(8,128)}, u32[]{:S(2)}) copy-start(f32[128,32]{0,1:T(8,128)} %multiply_reduce_fusion) | copy-start | bytes 49156
  335.1 16.0 %copy-start.13 = (f32[32,128]{1,0:T(8,128)S(1)}, f32[32,128]{1,0:T(8,128)}, u32[]{:S(2)}) copy-start(f32[32,128]{1,0:T(8,128)} %multiply_bitcast_fusion.1) | copy-start | bytes 49156
  341.0 0.8 copy-start.5
  347.1 11.3 %all-to-all-start.2 = ((bf16[128,32,1]{0,2,1:T(2,128)(2,1)}), bf16[128,32,1]{0,2,1:T(2,128)(2,1)S(1)}, u32[]{:S(2)}, u32[]{:S(2)}) async-start(bf16[128,32,1]{0,2,1:T(2,128)(2,1)} %copy.101), calls=%async_computation.2 | async-start | bytes 32768 | tf_op jit(solution)/shard_map/all_to_all | solution.py:161
  355.0 20.3 %copy-start.3 = (bf16[64,64,64]{2,1,0:T(8,128)(2,1)S(1)}, bf16[64,64,64]{2,1,0:T(8,128)(2,1)}, u32[]{:S(2)}) copy-start(bf16[64,64,64]{2,1,0:T(8,128)(2,1)} %copy.109) | copy-start | bytes 1572868
  358.5 14.5 %all-to-all-start.5 = ((bf16[128,32,1]{0,2,1:T(2,128)(2,1)}), bf16[128,32,1]{0,2,1:T(2,128)(2,1)}, u32[]{:S(2)}, u32[]{:S(2)}) async-start(bf16[128,32,1]{0,2,1:T(2,128)(2,1)} %copy.105), calls=%async_computation.5 | async-start | bytes 32768 | tf_op jit(solution)/shard_map/all_to_all | solution.py:160
  378.9 2.5 copy-start.1
  378.9 2.5 copy-start.10
  381.4 3.7 copy-start.17
  385.1 339.8 %copy-start.11 = (f32[64,64]{1,0:T(8,128)S(1)}, f32[64,64]{1,0:T(8,128)}, u32[]{:S(2)}) copy-start(f32[64,64]{1,0:T(8,128)} %mul.296) | copy-start | bytes 49156
  385.1 339.8 %copy-start.14 = (pred[64,64]{1,0:T(8,128)(4,1)S(1)}, pred[64,64]{1,0:T(8,128)(4,1)}, u32[]{:S(2)}) copy-start(pred[64,64]{1,0:T(8,128)(4,1)} %iota_compare_fusion.2) | copy-start | bytes 12292
Sparse Core Ops, SparseCore 0:
  11.2 68.2 all-gather.6
  90.9 57.2 all-gather.10
  151.3 61.4 all-gather.8
